TPU v7x, 256 devices: a whole 4x4x8 slice. The times are simulated.
256 devices in a mesh: seq: 16 (over x_hi, y, core), head: 16 (over x_lo, z).
Axes of the slice: x: 4 (x_hi: 2, x_lo: 2; x = x_hi * 2 + x_lo), y: 4, z: 8, core: 2. Of those that a mesh axis runs over, the one named last changes fastest.
Arguments:
- grad_out: bfloat16 [4096, 8192], P('seq', 'head'), may hold values from -6 to 6
- out_weight: bfloat16 [16384, 8192], P('head', 'seq'), may hold values from -0.046875 to 0.046875
- ssm_input: bfloat16 [4096, 16384], P('seq', 'head'), may hold values from -6 to 6
- step_size: float32 [4096, 128], P('seq', 'head'), may hold values from 0.02 to 0.2
- log_decay: float32 [4096, 128], P('seq', 'head'), may hold values from -1 to 0, as said below
- b_in: bfloat16 [4096, 256], P('seq'), may hold values from -1.5 to 1.5
- c_in: bfloat16 [4096, 256], P('seq'), may hold values from -1.5 to 1.5
- skip: float32 [128], P('head'), may hold values from 0.5 to 1.5
Outputs:
- grad_input: bfloat16 [4096, 16384], P('seq', 'head')
- grad_step: float32 [4096, 128], P('seq', 'head')
- grad_decay: float32 [4096, 128], P('seq', 'head')
- grad_b: float32 [4096, 256], P('seq')
- grad_c: float32 [4096, 256], P('seq')
Inputs may be any that keep to these rules, and one draw needn't show every extreme that they name: `log_decay`: every entry is negative.
All inputs are finite; a program needn't handle non-finite values.
Results may differ from a plain program's by a relative error of at most 0.0049.
Values may be sent and summed in bfloat16 or wider, within the bound.
A program may use at most 64 MiB of HBM per device.

v0:
```python
import jax
import jax.numpy as jnp
from jax import lax
from jax.sharding import PartitionSpec as P

HIGH = lax.Precision.HIGHEST


def entering(part, axis, combine, identity, reverse):
    count = lax.axis_size(axis)
    place = lax.axis_index(axis)
    ahead = count - 1 - place if reverse else place
    gathered = jax.tree.map(lambda a: lax.all_gather(a, axis), part)
    state = jax.tree.map(lambda a, e: jnp.zeros_like(a) + jnp.asarray(e, a.dtype), part, identity)

    def one(hop, state):
        source = count - 1 - hop if reverse else hop
        return combine(
            state, jax.tree.map(lambda a: lax.dynamic_index_in_dim(a, source, 0, False), gathered)
        )

    return lax.fori_loop(0, ahead, one, state)


def inner_terms(inputs, strides, running, b_rows, c_rows, skips):
    span = inputs.shape[0]
    row_pos = lax.broadcasted_iota(jnp.int32, (span, span), 0)
    col_pos = lax.broadcasted_iota(jnp.int32, (span, span), 1)
    causal = row_pos >= col_pos
    running_t = running.T
    gaps = running_t[:, :, None] - running_t[:, None, :]
    weights = jnp.exp(jnp.where(causal[None], gaps, -jnp.inf)) * strides.T[:, None, :]
    intersection = jnp.dot(c_rows, b_rows.T, precision=HIGH)
    mixed_sum = jnp.einsum("hts,shp->thp", weights * intersection[None], inputs, precision=HIGH)
    return mixed_sum + skips[None, :, None] * inputs


def carried(c_rows, running, carried_state):
    readout = jnp.einsum("tn,hpn->thp", c_rows, carried_state, precision=HIGH)
    return readout * jnp.exp(running)[:, :, None]


def closing(inputs, strides, b_rows, running, carried_state):
    block_end = running[-1]
    input_scale = strides * jnp.exp(block_end[None, :] - running)
    fresh = jnp.einsum("thp,tn->hpn", inputs * input_scale[:, :, None], b_rows, precision=HIGH)
    return jnp.exp(block_end)[:, None, None] * carried_state + fresh


def block_forward(inputs, strides, decays, b_rows, c_rows, skips, carried_state):
    running = jnp.cumsum(decays, axis=0)
    outputs = inner_terms(inputs, strides, running, b_rows, c_rows, skips) + carried(
        c_rows, running, carried_state
    )
    return (outputs, closing(inputs, strides, b_rows, running, carried_state))


def compose(first_part, second_part):
    return (
        first_part[0] * second_part[0],
        second_part[0][:, None, None] * first_part[1] + second_part[1],
    )


def local(grad_out, out_weight, ssm_input, step_size, log_decay, b_in, c_in, skip):
    full_grad = lax.all_gather(grad_out, "head", axis=1, tiled=True)
    span = ssm_input.shape[0]
    head_count = step_size.shape[1]
    head_width = ssm_input.shape[1] // head_count
    state_count = b_in.shape[1]
    grad_y = lax.dot_general(
        full_grad,
        lax.all_gather(out_weight, "seq", axis=1, tiled=True),
        (((1,), (1,)), ((), ())),
        preferred_element_type=jnp.float32,
    ).astype(jnp.bfloat16)
    inputs = ssm_input.astype(jnp.float32).reshape(span, head_count, head_width)
    upstream = grad_y.astype(jnp.float32).reshape(span, head_count, head_width)
    b_float = b_in.astype(jnp.float32)
    c_float = c_in.astype(jnp.float32)
    zero_state = jnp.zeros((head_count, head_width, state_count), jnp.float32)
    running = jnp.cumsum(log_decay, axis=0)
    block_decay = jnp.exp(running[-1])
    local_states = closing(inputs, step_size, b_float, running, zero_state)
    local_grads = jnp.einsum(
        "thp,tn->hpn", upstream * jnp.exp(running)[:, :, None], c_float, precision=HIGH
    )
    identity = (jnp.ones((head_count,), jnp.float32), jnp.zeros_like(zero_state))
    incoming = entering((block_decay, local_states), "seq", compose, identity, False)[1]
    outgoing = entering((block_decay, local_grads), "seq", compose, identity, True)[1]

    def forward_full(inputs_v, strides_v, decays_v, b_rows, c_rows):
        return block_forward(inputs_v, strides_v, decays_v, b_rows, c_rows, skip, incoming)

    pull_full = jax.vjp(forward_full, inputs, step_size, log_decay, b_float, c_float)[1]
    gradients = pull_full((upstream, outgoing))
    grad_b, grad_c = lax.psum((gradients[3], gradients[4]), "head")
    grad_input = gradients[0].reshape(span, head_count * head_width).astype(jnp.bfloat16)
    return (grad_input, gradients[1], gradients[2], grad_b, grad_c)


def solution(mesh):
    in_specs = (
        P("seq", "head"),
        P("head", "seq"),
        P("seq", "head"),
        P("seq", "head"),
        P("seq", "head"),
        P("seq", None),
        P("seq", None),
        P("head"),
    )
    out_specs = (
        P("seq", "head"),
        P("seq", "head"),
        P("seq", "head"),
        P("seq", None),
        P("seq", None),
    )
    return jax.shard_map(local, mesh=mesh, in_specs=in_specs, out_specs=out_specs, check_vma=False)
```

profile of v0, /device:TPU:8, one launch (start us, length us, event | category | flops | bytes accessed | tf_op | source)
XLA Modules:
  0.0 649.4 jit_solution(1202185131992663605)
XLA Ops:
  10.2 79.4 %all-gather.8.cloned.1.call-done = bf16[256,8192]{1,0:T(8,128)(2,1)} async-done(((bf16[256,512]{1,0:T(8,128)(2,1)}), bf16[256,8192]{1,0:T(8,128)(2,1)}) %all-gather.8.cloned.1.call-update) | async-done | bytes 4194320 | tf_op jit(solution)/shard_map/all_gather | solution.py:66
  89.6 122.1 %all-gather.10.cloned.1.call-done = bf16[1024,8192]{1,0:T(8,128)(2,1)} async-done(((bf16[1024,512]{1,0:T(8,128)(2,1)}), bf16[1024,8192]{1,0:T(8,128)(2,1)}) %all-gather.10.cloned.1.call-update) | async-done | bytes 16777232 | tf_op jit(solution)/shard_map/all_gather | solution.py:73
  211.7 11.6 %convolution_convert_fusion = bf16[256,1024]{1,0:T(8,128)(2,1)S(1)} fusion(bf16[256,8192]{1,0:T(8,128)(2,1)} %all-gather.8.cloned.1.call-done, bf16[1024,8192]{1,0:T(8,128)(2,1)} %all-gather.10.cloned.1.call-done), kind=kOutput, calls=%fused_computation.22 | convolution fusion | flops 4295229440 | bytes 21495808 | tf_op jit(solution)/shard_map/dot_general | solution.py:71
  224.2 1.7 fusion.15
  226.3 21.3 %all-gather.2 = f32[16,1,8]{2,1,0:T(1,128)S(1)} all-gather(f32[1,1,8]{2,1,0:T(1,128)S(1)} %bitcast.129), channel_id=1, replica_groups=mesh['seq'=16,'head'=16] {'seq'}, dimensions={0}, use_global_device_ids=true | all-gather | bytes 544 | tf_op jit(solution)/shard_map/all_gather | solution.py:13
  248.5 1.6 fusion.18
  250.1 88.0 %all-gather.12.cloned.1.call-done = f32[128,128,256]{2,1,0:T(8,128)} async-done(((f32[8,128,256]{2,1,0:T(8,128)}), f32[128,128,256]{2,1,0:T(8,128)}) %all-gather.12.cloned.1.call-update) | async-done | bytes 16777232 | tf_op jit(solution)/shard_map/all_gather | solution.py:13
  338.2 20.5 %while.26 = (s32[]{:T(128)}, f32[8,128,256]{2,1,0:T(8,128)S(1)}, s32[]{:T(128)}, f32[16,8]{1,0:T(8,128)S(1)}, f32[16,8,128,256]{3,2,1,0:T(8,128)}, /*index=5*/s32[]{:T(128)}, s32[]{:T(128)}, s32[]{:T(128)}, s32[]{:T(128)}) while((s32[]{:T(128)}, f32[8,128,256]{2,1,0:T(8,128)S(1)}, s32[]{:T(128)}, f32[16,8]{1,0:T(8,128)S(1)}, ...), condition=%wide.region_3.4_spmd, body=%wide.region_2.3_spmd.sunk | while | flops 524294 | bytes 3145979 | solution.py:22
  338.2 1.5 bitcast_add_fusion.6
  350.8 1.5 bitcast_add_fusion.6
  354.0 1.5 bitcast_add_fusion.6
  357.1 1.5 bitcast_add_fusion.6
  358.7 1.7 fusion.21
  361.7 1.7 convolution_add_fusion
  363.6 3.8 fusion.10
  367.4 2.0 copy.70
  369.5 1.8 fusion.20
  372.4 104.9 %all-gather.14.cloned.1.call-done = f32[128,128,256]{2,1,0:T(8,128)} async-done(((f32[8,128,256]{2,1,0:T(8,128)}), f32[128,128,256]{2,1,0:T(8,128)}) %all-gather.14.cloned.1.call-update) | async-done | bytes 16777232 | tf_op jit(solution)/shard_map/all_gather | solution.py:13
  477.4 3.2 while.27
  481.5 1.8 fusion.19
  484.5 2.5 reduce-window.16
  487.8 151.7 %all-reduce.4.cloned.1.call-done = (f32[256,256]{1,0:T(8,128)}, f32[256,256]{1,0:T(8,128)}) async-done(((f32[256,256]{1,0:T(8,128)}, f32[256,256]{1,0:T(8,128)}), (f32[256,256]{1,0:T(8,128)}, f32[256,256]{1,0:T(8,128)})) %all-reduce.4.cloned.1.call-update) | async-done | bytes 524304 | tf_op jit(solution)/shard_map/psum | solution.py:97
  639.5 1.7 copy.107
  641.2 1.7 copy.108
  (80 shorter events, 28.0 us)
Async XLA Ops:
  7.2 241.1 %copy-start = (bf16[256,256]{1,0:T(8,128)(2,1)S(1)}, bf16[256,256]{1,0:T(8,128)(2,1)}, u32[]{:S(2)}) copy-start(bf16[256,256]{1,0:T(8,128)(2,1)} %param.17) | copy-start | bytes 393220
  7.2 82.4 %all-gather.8.cloned.1.call-start = ((), (), s32[]{:S(2)}) async-start(), calls=%async_computation | async-start | bytes 4456448 | tf_op jit(solution)/shard_map/all_gather | solution.py:66
  7.9 203.8 %all-gather.10.cloned.1.call-start = ((), (), s32[]{:S(2)}) async-start(), calls=%async_computation.1 | async-start | bytes 17825792 | tf_op jit(solution)/shard_map/all_gather | solution.py:73
  8.7 329.4 %all-gather.12.cloned.1.call-start = ((), (), s32[]{:S(2)}) async-start(), calls=%async_computation.2 | async-start | bytes 17825792 | tf_op jit(solution)/shard_map/all_gather | solution.py:13
  223.2 0.9 copy-start.1
  223.4 2.5 copy-start.2
  224.2 24.3 %copy-start.3 = (f32[256,8]{0,1:T(8,128)S(1)}, f32[256,8]{0,1:T(8,128)}, u32[]{:S(2)}) copy-start(f32[256,8]{0,1:T(8,128)} %param.15) | copy-start | bytes 24580
  225.8 251.5 %all-gather.14.cloned.1.call-start = ((), (), s32[]{:S(2)}) async-start(), calls=%async_computation.3 | async-start | bytes 17825792 | tf_op jit(solution)/shard_map/all_gather | solution.py:13
  226.3 23.8 %copy-start.4 = (f32[8]{0:T(128)}, f32[8]{0:T(128)S(1)}, u32[]{:S(2)}) copy-start(f32[8]{0:T(128)S(1)} %get-tuple-element.199) | copy-start | bytes 100
  358.7 1.7 copy-start.5
  358.7 3.0 copy-start.7
  363.4 276.2 %all-reduce.4.cloned.1.call-start = ((), (), s32[]{:S(2)}) async-start(), calls=%async_computation.4 | async-start | bytes 1048576 | tf_op jit(solution)/shard_map/psum | solution.py:97
  363.6 5.8 copy-start.6
Sparse Core Ops, SparseCore 0:
  9.8 79.7 all-gather.7
  92.2 119.4 all-gather.9
  226.0 112.0 all-gather.11
  363.5 113.8 all-gather.13
  484.6 154.9 all-reduce.3
where the time goes:
time: 650 us; the launch traced here: 649 us
  waiting for transfers between devices  548 us (84%)
  other arithmetic  29.9 us (5%)
  matrix products  28.4 us (4%)
  blocking collectives  21.3 us (3%)
  between operations  14 us (2%)
  local copies, waits for them, and re-layouts  7.42 us (1%)
    all_gather x2, waiting for transfers between devices, entering(): gathered = jax.tree.map(lambda a: lax.all_gather(a, axis), part)  193 us
    psum x1, waiting for transfers between devices, local(): grad_b, grad_c = lax.psum((gradients[3], gradients[4]), 'head')  152 us
    all_gather x1, waiting for transfers between devices, local(): lax.all_gather(out_weight, 'seq', axis=1, tiled=True)  122 us
    all_gather x1, waiting for transfers between devices, local(): full_grad = lax.all_gather(grad_out, 'head', axis=1, tiled=True)  79.4 us
    add x15, other arithmetic, compose(): second_part[0][:, None, None] * first_part[1] + second_part[1]  23 us
    all_gather x1, blocking collectives, entering(): gathered = jax.tree.map(lambda a: lax.all_gather(a, axis), part)  21.3 us
  transfers between devices with their start and end apart: 5, of which 5 were waited for; matrix products, arithmetic and copies ran while one was open for 3% of the time, Pallas kernels for 0%

commit v1 on v0

--- a/solution.py
+++ b/solution.py
@@ -63,7 +63,9 @@
 
 
 def local(grad_out, out_weight, ssm_input, step_size, log_decay, b_in, c_in, skip):
-    full_grad = lax.all_gather(grad_out, "head", axis=1, tiled=True)
+    full_grad = jnp.concatenate(
+        lax.all_to_all(jnp.stack([grad_out] * lax.axis_size("head")), "head", 0, 0), axis=1
+    )
     span = ssm_input.shape[0]
     head_count = step_size.shape[1]
     head_width = ssm_input.shape[1] // head_count

time: 650 us -> 606 us (0.932)
  waiting for transfers between devices: 548 us -> 491 us
  starting transfers between devices: 0.38 us -> 10 us
    all_to_all x0 -> x1, waiting for transfers between devices: none -> 94.4 us  [local(): lax.all_to_all(jnp.stack([grad_out] * lax.axis_size('head')), 'head', 0, 0)]
    all_gather x1 -> x0, waiting for transfers between devices: 79.4 us -> none  [local(): full_grad = lax.all_gather(grad_out, 'head', axis=1, tiled=True)]
    all_gather x1, waiting for transfers between devices: 122 us -> 45.6 us  [local(): lax.all_gather(out_weight, 'seq', axis=1, tiled=True)]
    all_to_all x0 -> x1, starting transfers between devices: none -> 9.68 us  [local(): lax.all_to_all(jnp.stack([grad_out] * lax.axis_size('head')), 'head', 0, 0)]
where the time goes in v1:
time: 606 us; the launch traced here: 605 us
  waiting for transfers between devices  491 us (81%)
  other arithmetic  29.2 us (5%)
  matrix products  28.5 us (5%)
  blocking collectives  21.4 us (4%)
  between operations  14 us (2%)
  local copies, waits for them, and re-layouts  10.9 us (2%)
  starting transfers between devices  10 us (2%)
    all_gather x2, waiting for transfers between devices, entering(): gathered = jax.tree.map(lambda a: lax.all_gather(a, axis), part)  198 us
    psum x1, waiting for transfers between devices, local(): grad_b, grad_c = lax.psum((gradients[3], gradients[4]), 'head')  152 us
    all_to_all x1, waiting for transfers between devices, local(): lax.all_to_all(jnp.stack([grad_out] * lax.axis_size('head')), 'head', 0, 0)  94.4 us
    all_gather x1, waiting for transfers between devices, local(): lax.all_gather(out_weight, 'seq', axis=1, tiled=True)  45.6 us
    add x15, other arithmetic, compose(): second_part[0][:, None, None] * first_part[1] + second_part[1]  23 us
    all_gather x1, blocking collectives, entering(): gathered = jax.tree.map(lambda a: lax.all_gather(a, axis), part)  21.4 us
  transfers between devices with their start and end apart: 5, of which 5 were waited for; matrix products, arithmetic and copies ran while one was open for 3% of the time, Pallas kernels for 0%

profile of v1, /device:TPU:8, one launch (start us, length us, event | category | flops | bytes accessed | tf_op | source)
XLA Modules:
  0.0 605.3 jit_solution(14814258555150777460)
XLA Ops:
  9.0 2.4 stack.2
  11.4 9.7 %all-to-all-start = ((bf16[16,256,512]{1,2,0:T(8,128)(2,1)}), bf16[16,256,512]{1,2,0:T(8,128)(2,1)}, u32[]{:S(2)}, u32[]{:S(2)}) async-start(bf16[16,256,512]{1,2,0:T(8,128)(2,1)} %stack.2), calls=%async_computation | async-start | bytes 8388608 | tf_op jit(solution)/shard_map/all_to_all | solution.py:67
  22.0 94.4 %all-to-all-done = bf16[16,256,512]{1,2,0:T(8,128)(2,1)} async-done(((bf16[16,256,512]{1,2,0:T(8,128)(2,1)}), bf16[16,256,512]{1,2,0:T(8,128)(2,1)}, u32[]{:S(2)}, u32[]{:S(2)}) %all-to-all-start) | async-done | bytes 4194336 | tf_op jit(solution)/shard_map/all_to_all | solution.py:67
  116.4 45.6 %all-gather.7.cloned.1.call-done = bf16[1024,8192]{1,0:T(8,128)(2,1)} async-done(((bf16[1024,512]{1,0:T(8,128)(2,1)}), bf16[1024,8192]{1,0:T(8,128)(2,1)}) %all-gather.7.cloned.1.call-update) | async-done | bytes 16777232 | tf_op jit(solution)/shard_map/all_gather | solution.py:75
  162.0 11.6 %convolution_convert_fusion = bf16[256,1024]{1,0:T(8,128)(2,1)S(1)} fusion(bf16[256,8192]{0,1:T(8,128)(2,1)} %bitcast.11, bf16[1024,8192]{1,0:T(8,128)(2,1)} %all-gather.7.cloned.1.call-done), kind=kOutput, calls=%fused_computation.22 | convolution fusion | flops 4295229440 | bytes 21495808 | tf_op jit(solution)/shard_map/dot_general | solution.py:73
  174.5 1.7 fusion.15
  176.7 21.4 %all-gather.2 = f32[16,1,8]{2,1,0:T(1,128)S(1)} all-gather(f32[1,1,8]{2,1,0:T(1,128)S(1)} %bitcast.132), channel_id=1, replica_groups=mesh['seq'=16,'head'=16] {'seq'}, dimensions={0}, use_global_device_ids=true | all-gather | bytes 544 | tf_op jit(solution)/shard_map/all_gather | solution.py:13
  198.9 1.6 fusion.18
  200.5 93.5 %all-gather.9.cloned.1.call-done = f32[128,128,256]{2,1,0:T(8,128)} async-done(((f32[8,128,256]{2,1,0:T(8,128)}), f32[128,128,256]{2,1,0:T(8,128)}) %all-gather.9.cloned.1.call-update) | async-done | bytes 16777232 | tf_op jit(solution)/shard_map/all_gather | solution.py:13
  294.1 20.5 %while.26 = (s32[]{:T(128)}, f32[8,128,256]{2,1,0:T(8,128)S(1)}, s32[]{:T(128)}, f32[16,8]{1,0:T(8,128)S(1)}, f32[16,8,128,256]{3,2,1,0:T(8,128)}, /*index=5*/s32[]{:T(128)}, s32[]{:T(128)}, s32[]{:T(128)}, s32[]{:T(128)}) while((s32[]{:T(128)}, f32[8,128,256]{2,1,0:T(8,128)S(1)}, s32[]{:T(128)}, f32[16,8]{1,0:T(8,128)S(1)}, ...), condition=%wide.region_3.4_spmd, body=%wide.region_2.3_spmd.sunk | while | flops 524294 | bytes 3145979 | solution.py:22
  294.1 1.5 bitcast_add_fusion.6
  297.3 1.5 bitcast_add_fusion.6
  314.6 1.7 fusion.21
  317.6 1.7 convolution_add_fusion
  319.5 3.8 fusion.10
  323.3 2.0 copy.73
  325.4 1.8 fusion.20
  328.3 104.9 %all-gather.11.cloned.1.call-done = f32[128,128,256]{2,1,0:T(8,128)} async-done(((f32[8,128,256]{2,1,0:T(8,128)}), f32[128,128,256]{2,1,0:T(8,128)}) %all-gather.11.cloned.1.call-update) | async-done | bytes 16777232 | tf_op jit(solution)/shard_map/all_gather | solution.py:13
  433.4 3.2 while.27
  437.4 1.8 fusion.19
  440.4 2.5 reduce-window.16
  443.7 151.7 %all-reduce.4.cloned.1.call-done = (f32[256,256]{1,0:T(8,128)}, f32[256,256]{1,0:T(8,128)}) async-done(((f32[256,256]{1,0:T(8,128)}, f32[256,256]{1,0:T(8,128)}), (f32[256,256]{1,0:T(8,128)}, f32[256,256]{1,0:T(8,128)})) %all-reduce.4.cloned.1.call-update) | async-done | bytes 524304 | tf_op jit(solution)/shard_map/psum | solution.py:99
  595.4 1.7 copy.110
  597.1 1.7 copy.111
  (83 shorter events, 30.8 us)
Async XLA Ops:
  7.2 191.5 %copy-start = (bf16[256,256]{1,0:T(8,128)(2,1)S(1)}, bf16[256,256]{1,0:T(8,128)(2,1)}, u32[]{:S(2)}) copy-start(bf16[256,256]{1,0:T(8,128)(2,1)} %param.17) | copy-start | bytes 393220
  7.2 154.8 %all-gather.7.cloned.1.call-start = ((), (), s32[]{:S(2)}) async-start(), calls=%async_computation.1 | async-start | bytes 17825792 | tf_op jit(solution)/shard_map/all_gather | solution.py:75
  11.4 9.7 %copy-start.4 = (f32[256,8]{0,1:T(8,128)S(1)}, f32[256,8]{0,1:T(8,128)}, u32[]{:S(2)}) copy-start(f32[256,8]{0,1:T(8,128)} %param.16) | copy-start | bytes 24580
  11.4 105.0 %all-to-all-start = ((bf16[16,256,512]{1,2,0:T(8,128)(2,1)}), bf16[16,256,512]{1,2,0:T(8,128)(2,1)}, u32[]{:S(2)}, u32[]{:S(2)}) async-start(bf16[16,256,512]{1,2,0:T(8,128)(2,1)} %stack.2), calls=%async_computation | async-start | bytes 8388608 | tf_op jit(solution)/shard_map/all_to_all | solution.py:67
  21.1 272.9 %all-gather.9.cloned.1.call-start = ((), (), s32[]{:S(2)}) async-start(), calls=%async_computation.2 | async-start | bytes 17825792 | tf_op jit(solution)/shard_map/all_gather | solution.py:13
  173.6 0.9 copy-start.1
  173.7 2.5 copy-start.2
  174.5 24.4 %copy-start.3 = (f32[256,8]{0,1:T(8,128)S(1)}, f32[256,8]{0,1:T(8,128)}, u32[]{:S(2)}) copy-start(f32[256,8]{0,1:T(8,128)} %param.15) | copy-start | bytes 24580
  176.2 257.1 %all-gather.11.cloned.1.call-start = ((), (), s32[]{:S(2)}) async-start(), calls=%async_computation.3 | async-start | bytes 17825792 | tf_op jit(solution)/shard_map/all_gather | solution.py:13
  176.7 23.8 %copy-start.5 = (f32[8]{0:T(128)}, f32[8]{0:T(128)S(1)}, u32[]{:S(2)}) copy-start(f32[8]{0:T(128)S(1)} %get-tuple-element.199) | copy-start | bytes 100
  314.6 1.7 copy-start.6
  314.6 3.0 copy-start.8
  319.3 276.1 %all-reduce.4.cloned.1.call-start = ((), (), s32[]{:S(2)}) async-start(), calls=%async_computation.4 | async-start | bytes 1048576 | tf_op jit(solution)/shard_map/psum | solution.py:99
  319.5 5.8 copy-start.7
Sparse Core Ops, SparseCore 0:
  10.6 151.3 all-gather.6
  176.3 117.6 all-gather.8
  319.4 113.8 all-gather.10
  440.5 154.8 all-reduce.3
